TPU v7x, 128 devices: a whole 4x4x4 slice. The times are simulated.
128 devices in a mesh: row: 16 (over y, x), col: 8 (over z, core).
Axes of the slice: x: 4, y: 4, z: 4, core: 2. Of those that a mesh axis runs over, the one named last changes fastest.
Arguments:
- panel: float32 [32768, 256], P('row', 'col'), may hold values from -60 to 60
- trailing_in: float32 [32768, 10240], P('row', 'col'), may hold values from -60 to 60
Outputs:
- r_factor: float32 [256, 256], replicated
- q_panel: float32 [32768, 256], P('row')
- r_trail: float32 [256, 10240], P(None, 'col')
- trailing_out: float32 [32768, 10240], P('row', 'col')
All inputs are finite; a program needn't handle non-finite values.
Results may differ from a plain program's by a relative error of at most 0.00012.
Values sent between devices are 32-bit elements; how exact they have to be, the bound alone decides.
A program may use at most 128 MiB of HBM per device.

v0:
```python
import math

import jax
import jax.numpy as jnp
from jax import lax
from jax.sharding import PartitionSpec as P


def upper_of(gram):
    return jnp.linalg.cholesky(gram).T


def inverse_lower(upper_r, panel_width):
    identity = jnp.eye(panel_width, dtype=jnp.float32)
    return jax.scipy.linalg.solve_triangular(upper_r.T, identity, lower=True)


def per_device(panel, trailing_in):
    highest = lax.Precision.HIGHEST
    whole_panel = lax.all_gather(panel, "col", axis=1, tiled=True)
    rows_all = whole_panel.shape[0] * lax.axis_size("row")
    panel_width = whole_panel.shape[1]
    inv_root = 1.0 / math.sqrt(rows_all)
    local_gram = jnp.dot(whole_panel.T, whole_panel, precision=highest) / rows_all
    summed = lax.psum(local_gram, "row")
    upper_r = upper_of(summed)
    l_inverse = inverse_lower(upper_r, panel_width)
    q_panel = jnp.dot(whole_panel, l_inverse.T, precision=highest)
    local_terms = jnp.dot(q_panel.T, trailing_in, precision=highest)
    r_trail = lax.psum(local_terms, "row") * inv_root
    trailing_out = trailing_in - jnp.dot(q_panel, r_trail, precision=highest) * inv_root
    return (upper_r, q_panel, r_trail, trailing_out)


def solution(mesh):
    in_specs = (P("row", "col"), P("row", "col"))
    out_specs = (P(), P("row", None), P(None, "col"), P("row", "col"))
    return jax.shard_map(
        per_device, mesh=mesh, in_specs=in_specs, out_specs=out_specs, check_vma=False
    )
```

profile of v0, /device:TPU:0, one launch (start us, length us, event | category | flops | bytes accessed | tf_op | source)
XLA Modules:
  0.0 315.4 jit_solution(15138777126609384406)
XLA Ops:
  7.2 0.0 all-gather.2.cloned.1.call-start
  7.2 0.7 all-gather.2.cloned.1.call-update
  7.9 0.0 all-reduce.4.cloned.1.call-start
  7.9 29.8 %all-gather.2.cloned.1.call-done = f32[2048,256]{0,1:T(8,128)} async-done(((f32[2048,32]{0,1:T(8,128)}), f32[2048,256]{0,1:T(8,128)}) %all-gather.2.cloned.1.call-update) | async-done | bytes 2097168 | tf_op jit(solution)/shard_map/all_gather | solution.py:20
  37.7 4.8 %convolution_multiply_fusion = f32[256,256]{0,1:T(8,128)} fusion(f32[2048,256]{0,1:T(8,128)} %all-gather.2.cloned.1.call-done), kind=kOutput, calls=%fused_computation.3 | convolution fusion | flops 1610678272 | bytes 2359296 | tf_op jit(solution)/shard_map/dot_general | solution.py:24
  42.5 0.0 all-reduce.4.cloned.1.call-update
  42.5 0.0 all-reduce.6.cloned.1.call-start
  42.6 84.9 %all-reduce.4.cloned.1.call-done = f32[256,256]{0,1:T(8,128)} async-done(((f32[256,256]{0,1:T(8,128)}), f32[256,256]{0,1:T(8,128)}) %all-reduce.4.cloned.1.call-update) | async-done | bytes 262160 | tf_op jit(solution)/shard_map/psum | solution.py:25
  127.6 1.1 copy.7
  128.6 1.0 fusion.4
  129.7 11.7 %cholesky.50 = f32[128,128]{1,0:T(8,128)S(1)} custom-call(f32[128,128]{1,0:T(8,128)S(1)} %cholesky.118), custom_call_target="Cholesky" | custom-call | tf_op jit(solution)/shard_map/jit(cholesky)/cholesky | solution.py:10
  141.4 9.8 %custom-call.15 = f32[1,128,128]{1,2,0:T(8,128)S(1)} custom-call(f32[1,128,128]{2,1,0:T(8,128)S(1)} %get-tuple-element.31), custom_call_target="InvertDiagBlocksLowerTriangular" | custom-call | tf_op jit(solution)/shard_map/jit(cholesky)/cholesky | solution.py:10
  151.2 0.2 constant_dynamic-update-slice_fusion.1
  151.5 0.3 convolution_subtract_fusion.1
  151.7 11.7 %cholesky.105 = f32[128,128]{1,0:T(8,128)S(1)} custom-call(f32[128,128]{1,0:T(8,128)S(1)} %convolution_subtract_fusion.1), custom_call_target="Cholesky" | custom-call | tf_op jit(solution)/shard_map/jit(cholesky)/cholesky | solution.py:10
  163.5 0.6 compare_reduce_fusion
  165.5 0.1 triangular_solve.44
  165.5 4.1 %while.1 = (s32[]{:T(128)}, f32[256,256]{1,0:T(8,128)S(1)}, s32[2,2]{1,0:T(2,128)S(1)}, f32[2,128,128]{2,1,0:T(8,128)S(1)}, s32[]{:T(128)}) while((s32[]{:T(128)}, f32[256,256]{1,0:T(8,128)S(1)}, s32[2,2]{1,0:T(2,128)S(1)}, f32[2,128,128]{2,1,0:T(8,128)S(1)}, s32[]{:T(128)}) %tuple.29), condition=%wide.while_cond, body=%wide.while_body.sunk | while | flops 2 | bytes 131189 | solution.py:15
  165.7 0.6 fusion.29
  166.3 1.4 bitcast_dynamic-update-slice_fusion.2
  167.7 0.6 fusion.29
  168.3 1.4 bitcast_dynamic-update-slice_fusion.2
  169.7 19.7 %custom-call.16 = f32[2,128,128]{1,2,0:T(8,128)S(1)} custom-call(f32[2,128,128]{2,1,0:T(8,128)S(1)} %get-tuple-element.11), custom_call_target="InvertDiagBlocksLowerTriangular" | custom-call | tf_op jit(solution)/shard_map/jit(_solve_triangular)/triangular_solve | solution.py:15
  189.3 0.3 fusion.7
  189.6 0.3 convolution_subtract_fusion
  189.9 0.3 fusion.10
  190.2 3.5 %fusion = f32[256,2048]{1,0:T(8,128)S(1)} fusion(f32[2048,256]{0,1:T(8,128)} %all-gather.2.cloned.1.call-done, f32[128,256]{1,0:T(8,128)S(1)} %fusion.10, f32[128,256]{1,0:T(8,128)S(1)} %fusion.7), kind=kOutput, calls=%fused_computation.7 | convolution fusion | flops 1610678272 | bytes 4456448 | tf_op jit(solution)/shard_map/dot_general | solution.py:28
  193.7 12.7 %fusion.16 = f32[256,1280]{1,0:T(8,128)} fusion(f32[256,2048]{1,0:T(8,128)S(1)} %fusion, f32[2048,1280]{1,0:T(8,128)} %param.3), kind=kOutput, calls=%fused_computation.39 | convolution fusion | flops 8053063680 | bytes 13893632 | tf_op jit(solution)/shard_map/dot_general | solution.py:29
  206.3 0.0 all-reduce.6.cloned.1.call-update
  206.4 0.8 copy.8
  207.2 1.8 copy.9
  209.0 84.8 %all-reduce.6.cloned.1.call-done = f32[256,1280]{1,0:T(8,128)} async-done(((f32[256,1280]{1,0:T(8,128)}), f32[256,1280]{1,0:T(8,128)}) %all-reduce.6.cloned.1.call-update) | async-done | bytes 1310736 | tf_op jit(solution)/shard_map/psum | solution.py:30
  293.8 1.4 broadcast_multiply_fusion
  295.2 0.0 copy-start
  295.2 13.6 %multiply_subtract_fusion = f32[2048,1280]{1,0:T(8,128)} fusion(f32[2048,1280]{1,0:T(8,128)} %param.3, f32[256,2048]{1,0:T(8,128)S(1)} %fusion, f32[256,1280]{1,0:T(8,128)S(1)} %broadcast_multiply_fusion), kind=kOutput, calls=%fused_computation.2 | convolution fusion | flops 8058306560 | bytes 24379392 | tf_op jit(solution)/shard_map/dot_general | solution.py:31
  308.9 0.0 copy-done
  (10 shorter events, 0.2 us)
Async XLA Ops:
  7.2 30.6 %all-gather.2.cloned.1.call-start = ((), (), s32[]{:S(2)}) async-start(), calls=%async_computation | async-start | bytes 2359296 | tf_op jit(solution)/shard_map/all_gather | solution.py:20
  7.9 119.7 %all-reduce.4.cloned.1.call-start = ((), (), s32[]{:S(2)}) async-start(), calls=%async_computation.1 | async-start | bytes 524288 | tf_op jit(solution)/shard_map/psum | solution.py:25
  42.5 251.3 %all-reduce.6.cloned.1.call-start = ((), (), s32[]{:S(2)}) async-start(), calls=%async_computation.2 | async-start | bytes 2621440 | tf_op jit(solution)/shard_map/psum | solution.py:30
  295.2 13.6 %copy-start = (f32[256,1280]{1,0:T(8,128)}, f32[256,1280]{1,0:T(8,128)S(1)}, u32[]{:S(2)}) copy-start(f32[256,1280]{1,0:T(8,128)S(1)} %broadcast_multiply_fusion) | copy-start | bytes 3932164
Sparse Core Ops, SparseCore 0:
  9.7 27.9 all-gather.1
  42.7 84.8 all-reduce.3
  206.5 87.2 all-reduce.5
where the time goes:
time: 316 us; the launch traced here: 315 us
  waiting for transfers between devices  200 us (63%)
  other arithmetic  56.1 us (18%)
  matrix products  35.8 us (11%)
  between operations  15.2 us (5%)
  local copies, waits for them, and re-layouts  7.77 us (2%)
    psum x1, waiting for transfers between devices, per_device(): summed = lax.psum(local_gram, 'row')  84.9 us
    psum x1, waiting for transfers between devices, per_device(): r_trail = lax.psum(local_terms, 'row') * inv_root  84.8 us
    another operation x6, other arithmetic, upper_of(): return jnp.linalg.cholesky(gram).T  34 us
    all_gather x1, waiting for transfers between devices, per_device(): whole_panel = lax.all_gather(panel, 'col', axis=1, tiled=True)  29.8 us
    another operation x3, other arithmetic, inverse_lower(): return jax.scipy.linalg.solve_triangular(upper_r.T, identity, lower=True)  19.7 us
    dot_general x1, matrix products, per_device(): jnp.dot(q_panel, r_trail, precision=highest) * inv_root  13.6 us
    dot_general x1, matrix products, per_device(): local_terms = jnp.dot(q_panel.T, trailing_in, precision=highest)  12.7 us
  transfers between devices with their start and end apart: 3, of which 3 were waited for; matrix products, arithmetic and copies ran while one was open for 1% of the time, Pallas kernels for 0%

commit v1 on v0

v1 whole, which is shorter than its diff:
```python
import functools
import math

import jax
import jax.numpy as jnp
from jax import lax
from jax.experimental import pallas as pl
from jax.experimental.pallas import tpu as pltpu
from jax.sharding import PartitionSpec as P

F32 = jnp.float32
BF16 = jnp.bfloat16
NN = (((1,), (0,)), ((), ()))
NT = (((1,), (1,)), ((), ()))
TN = (((0,), (0,)), ((), ()))
BLOCK = 32
TILE = 256
dot = functools.partial(lax.dot_general, preferred_element_type=F32)


def split2(x):
    high = x.astype(BF16)
    return high, (x - high.astype(F32)).astype(BF16)


def split3(x):
    high = x.astype(BF16)
    rest = x - high.astype(F32)
    middle = rest.astype(BF16)
    return high, middle, (rest - middle.astype(F32)).astype(BF16)


def left3(x):
    high, low = split2(x)
    return jnp.concatenate([high, low, high], axis=1)


def right3(x, axis=0):
    high, low = split2(x)
    return jnp.concatenate([high, high, low], axis=axis)


def eliminate(r, at):
    groups = BLOCK // 8
    rows = lax.broadcasted_iota(jnp.int32, (8, 128), 0)
    base = (at // 128) * 128
    d = r[:, base : base + 128]
    cols = []
    for q in range(BLOCK):
        lane = at - base + q
        cols.append(
            {
                g: jnp.broadcast_to(d[8 * g : 8 * g + 8, lane : lane + 1], (8, 128))
                for g in range(q // 8, groups)
            }
        )
    width = r.shape[1] // 128
    rr = [
        [r[8 * g : 8 * g + 8, 128 * c : 128 * c + 128] for c in range(width)]
        for g in range(groups)
    ]

    def spread(v, s):
        return jnp.broadcast_to(v[s : s + 1, :], (8, 128))

    for p in range(BLOCK):
        gp, sp = p // 8, p % 8
        inverse = lax.rsqrt(spread(cols[p][gp], sp))
        column = {g: cols[p][g] * inverse for g in range(gp, groups)}
        for q in range(p + 1, BLOCK):
            b = spread(column[q // 8], q % 8)
            for g in range(q // 8, groups):
                cols[q][g] = cols[q][g] - column[g] * b
        below = dict(column)
        below[gp] = jnp.where(rows > sp, column[gp], 0.0)
        for c in range(width):
            row = spread(rr[gp][c], sp) * inverse
            for g in range(gp, groups):
                new = rr[g][c] - below[g] * row
                rr[g][c] = jnp.where(rows == sp, row, new) if g == gp else new
    return jnp.concatenate([jnp.concatenate(x, axis=1) for x in rr], axis=0)


def factor_stage(k, n, m_ref, u_ref, x_ref):
    o = k * BLOCK
    e = o + BLOCK
    r = eliminate(m_ref[o:e, :], o)
    at_row = lax.broadcasted_iota(jnp.int32, (BLOCK, n), 0) + o
    at_col = lax.broadcasted_iota(jnp.int32, (BLOCK, n), 1)
    u_ref[o:e, :] = jnp.where(at_col >= at_row, r[:, :n], 0.0)
    x_ref[o:e, :] = r[:, n:]
    if e < n:
        a0 = (e // 128) * 128
        h, m, l = split3(r)
        left = jnp.concatenate([h, h, m, h, l, m], axis=0)[:, a0:n]
        right = jnp.concatenate([h, m, h, l, h, m], axis=0)
        m_ref[e:n, :] = m_ref[e:n, :] - dot(left, right, TN)[e - a0 :, :]


def exchange_kernel(
    scale, batches, pan, tin, pt, tv, u, x, *rest,
):
    nb = len(batches)
    wf, rest = rest[:nb], rest[nb:]
    (ph, gb, gr, m, t_sem, own_sem, ps, pr, gs, grs, ws, wr), rest = rest[:12], rest[12:]
    wl, r1, r2, r3, r4 = (rest[nb * i : nb * i + nb] for i in range(5))
    n = pt.shape[0]
    rows = pt.shape[1]
    width = pan.shape[0]
    half = width // 2
    row, col = lax.axis_index("row"), lax.axis_index("col")
    y, xx = row // 4, row % 4
    z, core = col // 2, col % 2
    up, down = lax.rem(z + 1, 4), lax.rem(z + 3, 4)
    peer_up = (row, 2 * up + core)
    peer_down = (row, 2 * down + core)
    peer_core = (row, 2 * z + 1 - core)
    peers = (
        (4 * y + xx + 1 - 2 * (xx % 2), col),
        (4 * y + 3 - xx, col),
        (4 * (y + 1 - 2 * (y % 2)) + xx, col),
        (4 * (3 - y) + xx, col),
    )
    bits = ((xx + 1) // 2 % 2, xx // 2, (y + 1) // 2 % 2, y // 2)
    orders = ((0, 1, 2, 3), (1, 0, 3, 2), (2, 3, 0, 1), (3, 2, 1, 0))
    mesh = pl.DeviceIdType.MESH

    quarter = rows // 4
    loads = [
        pltpu.make_async_copy(tin.at[pl.ds(i * quarter, quarter)], tv.at[pl.ds(i * quarter, quarter)], t_sem.at[i])
        for i in range(4)
    ]
    own = pltpu.make_async_copy(pan, pt.at[pl.ds(width * col, width)], own_sem)
    own.start()
    barrier = pltpu.get_barrier_semaphore()
    for peer in (peer_up, peer_down, peer_core, *peers):
        pl.semaphore_signal(barrier, inc=1, device_id=peer, device_id_type=mesh)
    pl.semaphore_wait(barrier, 7)

    sent = []

    def send(src, dst, ssem, rsem, peer):
        copy = pltpu.make_async_remote_copy(src, dst, ssem, rsem, device_id=peer, device_id_type=mesh)
        copy.start()
        sent.append(copy)
        return copy

    def piece(c, part):
        return pt.at[pl.ds(width * c + half * part, half)]

    def forward(index, c, part, peer):
        return send(piece(c, part), piece(c, part), ps.at[index], pr.at[index], peer)

    p0 = send(pan.at[pl.ds(0, half)], piece(col, 0), ps.at[0], pr.at[0], peer_up)
    m0 = send(pan.at[pl.ds(half, half)], piece(col, 1), ps.at[1], pr.at[1], peer_down)
    p1 = send(pan.at[pl.ds(half, half)], piece(col, 1), ps.at[2], pr.at[2], peer_up)
    m1 = send(pan.at[pl.ds(0, half)], piece(col, 0), ps.at[3], pr.at[3], peer_down)
    c0 = send(pan, pt.at[pl.ds(width * col, width)], ps.at[4], pr.at[4], peer_core)
    for load in loads:
        load.start()
    c_down, c_up, c_far = 2 * down + core, 2 * up + core, 2 * lax.rem(z + 2, 4) + core
    p0.wait_recv()
    p2 = forward(5, c_down, 0, peer_up)
    f1 = forward(6, c_down, 0, peer_core)
    m0.wait_recv()
    m2 = forward(7, c_up, 1, peer_down)
    f2 = forward(8, c_up, 1, peer_core)
    p1.wait_recv()
    f3 = forward(9, c_down, 1, peer_core)
    m1.wait_recv()
    f4 = forward(10, c_up, 0, peer_core)
    p2.wait_recv()
    f5 = forward(11, c_far, 0, peer_core)
    m2.wait_recv()
    f6 = forward(12, c_far, 1, peer_core)
    own.wait()
    for copy in (c0, f1, f2, f3, f4, f5, f6):
        copy.wait_recv()

    whole = pt[...]
    ph[...] = left3(whole)
    gb[0] = dot(ph[...], right3(whole, 1), NT) * scale

    def gram_send(step):
        return [
            send(
                gb.at[step, pl.ds(64 * s, 64)], gr.at[step, pl.ds(64 * s, 64)],
                gs.at[step, s], grs.at[step, s], peers[orders[s][step]],
            )
            for s in range(4)
        ]

    def gram_add(step, copies):
        for s in range(4):
            at = slice(64 * s, 64 * s + 64)
            copies[s].wait_recv()
            if step < 3:
                gb[step + 1, at] = gb[step, at] + gr[step, at]
            else:
                m[at, :n] = gb[step, at] + gr[step, at]

    def product(b, i):
        j = batches[b][0] + i
        right = right3(tv[:, TILE * j : TILE * j + TILE])
        wl[b][:, TILE * i : TILE * i + TILE] = dot(ph[...], right, NN)

    kept, other = [], []
    for s in range(4):
        at = 64 * s
        k_s, o_s = [], []
        for level in range(3):
            size = 32 >> level
            b = bits[orders[s][level]]
            k_s.append(pl.multiple_of(at + size * b, 8))
            o_s.append(pl.multiple_of(at + size * (1 - b), 8))
            at = at + size * b
        kept.append(k_s)
        other.append(o_s)
    landing = (r1, r2, r3)
    flights = {}

    def product_send(b, level):
        copies = []
        for s in range(4):
            if level < 3:
                size = 32 >> level
                src = wl[b].at[pl.ds(other[s][level], size)]
                dst = landing[level][b].at[pl.ds(size * s, size)]
                axis = level
            elif level == 3:
                src = wl[b].at[pl.ds(kept[s][2], 8)]
                dst = r4[b].at[pl.ds(8 * s, 8)]
                axis = 3
            else:
                axis = 6 - level
                src = dst = wf[b].at[pl.ds(kept[s][axis], 32 >> axis)]
            copies.append(send(src, dst, ws.at[b, level, s], wr.at[b, level, s], peers[orders[s][axis]]))
        flights[b, level] = copies

    def product_step(b, level):
        for s in range(4):
            flights[b, level][s].wait_recv()
            if level < 3:
                size = 32 >> level
                at = pl.ds(kept[s][level], size)
                wl[b][at] = wl[b][at] + landing[level][b][size * s : size * s + size]
            elif level == 3:
                at = pl.ds(kept[s][2], 8)
                wf[b][at] = wl[b][at] + r4[b][8 * s : 8 * s + 8]
        if level < 6:
            product_send(b, level + 1)

    copies = gram_send(0)
    for load in loads:
        load.wait()
    product(0, 0)
    product(0, 1)
    gram_add(0, copies)
    copies = gram_send(1)
    product_send(0, 0)
    product(1, 0)
    product(1, 1)
    gram_add(1, copies)
    copies = gram_send(2)
    product(1, 2)
    product_send(1, 0)
    product_step(0, 0)
    gram_add(2, copies)
    copies = gram_send(3)
    product_step(1, 0)
    gram_add(3, copies)

    ri = lax.broadcasted_iota(jnp.int32, (n, n), 0)
    ci = lax.broadcasted_iota(jnp.int32, (n, n), 1)
    m[:, n:] = jnp.where(ri == ci, 1.0, 0.0).astype(F32)
    events = [(b, level) for level in range(1, 7) for b in (0, 1)]
    stages = n // BLOCK
    done = 0
    for k in range(stages):
        factor_stage(k, n, m, u, x)
        goal = (len(events) * (k + 1)) // stages
        while done < goal:
            product_step(*events[done])
            done += 1
    for copy in sent:
        copy.wait_send()


def exchange(panel_t, trailing, scale):
    width, rows = panel_t.shape
    n = width * 8
    tc = trailing.shape[1]
    batches = ((0, 2), (2, 5))
    widths = [TILE * (hi - lo) for lo, hi in batches]
    vm = pltpu.VMEM
    dma = pltpu.SemaphoreType.DMA
    return pl.pallas_call(
        functools.partial(exchange_kernel, scale, batches),
        out_shape=(vm((n, rows), F32), vm((rows, tc), F32), vm((n, n), F32), vm((n, n), F32), *(vm((n, c), F32) for c in widths)),
        in_specs=[pl.BlockSpec(memory_space=pltpu.HBM)] * 2,
        out_specs=(pl.BlockSpec(memory_space=pltpu.VMEM),) * (4 + len(batches)),
        scratch_shapes=[
            vm((n, 3 * rows), BF16),
            vm((4, n, n), F32),
            vm((4, n, n), F32),
            vm((n, 2 * n), F32),
            dma((4,)),
            dma,
            dma((13,)),
            dma((13,)),
            dma((4, 4)),
            dma((4, 4)),
            dma((2, 7, 4)),
            dma((2, 7, 4)),
            *(vm((size, c), F32) for size in (n, 128, 64, 32, 32) for c in widths),
        ],
        compiler_params=pltpu.CompilerParams(
            collective_id=0, has_side_effects=True, vmem_limit_bytes=36 * 2**20
        ),
        name="exchange",
    )(panel_t, trailing)


def update_kernel(inv_root, block, starts, pt, tv, u, x, *rest):
    ws, (u_out, q_out, r_out, t_out, r3, x3) = rest[:-6], rest[-6:]
    i = pl.program_id(0)

    @pl.when(i == 0)
    def _():
        left = left3(x[...])
        x3[...] = right3(x[...].T)
        for w, start in zip(ws, starts):
            for c in range(0, w.shape[1], TILE):
                r = dot(left, right3(w[:, c : c + TILE]), NN) * inv_root
                r_out[:, start + c : start + c + TILE] = r
                r3[:, start + c : start + c + TILE] = right3(r * inv_root)
        u_out[...] = u[...]

    at = pl.ds(pl.multiple_of(i * block, block), block)
    q = dot(left3(pt[:, at].T), x3[...], NN)
    q_out[...] = q
    q3 = left3(q)
    for c in range(0, r_out.shape[1], TILE):
        t_out[:, c : c + TILE] = tv[at, c : c + TILE] - dot(q3, r3[:, c : c + TILE], NN)


def update(pt, tv, u, x, ws, inv_root, block=256):
    n, rows = pt.shape
    tc = tv.shape[1]
    starts = [sum(w.shape[1] for w in ws[:i]) for i in range(len(ws))]
    resident = pl.BlockSpec(memory_space=pltpu.VMEM)

    def whole(*shape):
        return pl.BlockSpec(shape, lambda i: (0, 0))

    def by_rows(width):
        return pl.BlockSpec((block, width), lambda i: (i, 0))

    return pl.pallas_call(
        functools.partial(update_kernel, inv_root, block, starts),
        grid=(rows // block,),
        out_shape=(
            jax.ShapeDtypeStruct((n, n), F32),
            jax.ShapeDtypeStruct((rows, n), F32),
            jax.ShapeDtypeStruct((n, tc), F32),
            jax.ShapeDtypeStruct((rows, tc), F32),
        ),
        in_specs=[resident] * (4 + len(ws)),
        out_specs=(whole(n, n), by_rows(n), whole(n, tc), by_rows(tc)),
        scratch_shapes=[pltpu.VMEM((3 * n, tc), BF16), pltpu.VMEM((3 * n, n), BF16)],
        compiler_params=pltpu.CompilerParams(vmem_limit_bytes=20 * 2**20),
        name="update",
    )(pt, tv, u, x, *ws)


def per_device(panel, trailing_in):
    rows_all = panel.shape[0] * lax.axis_size("row")
    pt, tv, u, x, *ws = exchange(panel.T, trailing_in, 1.0 / rows_all)
    return update(pt, tv, u, x, ws, 1.0 / math.sqrt(rows_all))


def solution(mesh):
    in_specs = (P("row", "col"), P("row", "col"))
    out_specs = (P(), P("row", None), P(None, "col"), P("row", "col"))
    return jax.shard_map(
        per_device, mesh=mesh, in_specs=in_specs, out_specs=out_specs, check_vma=False
    )
```

time: 316 us -> 72 us (0.23)
  waiting for transfers between devices: 200 us -> 0 us
  Pallas kernels: 0 us -> 70.3 us
  other arithmetic: 56.1 us -> 0 us
  matrix products: 35.8 us -> 0 us
  between operations: 15.2 us -> 0.65 us
  local copies, waits for them, and re-layouts: 7.77 us -> 0.94 us
    psum x2 -> x0, waiting for transfers between devices: 170 us -> none  [the longest x1 84.9 us: per_device(): summed = lax.psum(local_gram, 'row')]
    pallas_call x0 -> x2, Pallas kernels: none -> 70.3 us  [the longest x1 59.6 us: exchange(): pl.pallas_call(functools.partial(exchange_kernel, scale, batches), out_sh...]
    another operation x9 -> x0, other arithmetic: 53.7 us -> none  [the longest x6 34 us: upper_of(): return jnp.linalg.cholesky(gram).T]
    dot_general x4 -> x0, matrix products: 34.5 us -> none  [the longest x1 13.6 us: per_device(): jnp.dot(q_panel, r_trail, precision=highest) * inv_root]
    all_gather x1 -> x0, waiting for transfers between devices: 29.8 us -> none  [per_device(): whole_panel = lax.all_gather(panel, 'col', axis=1, tiled=True)]
    another operation x9 -> x0, local copies, waits for them, and re-layouts: 4.05 us -> none
  transfers between devices with their start and end apart: 3 -> 0, of which waited for: 3 -> 0; matrix products, arithmetic and copies ran while one was open for 1% -> 0% of each run, Pallas kernels for 0% -> 0%
where the time goes in v1:
time: 72 us; the launch traced here: 71.9 us
  Pallas kernels  70.3 us (98%)
  local copies, waits for them, and re-layouts  0.94 us (1%)
    pallas_call x1, Pallas kernels, exchange(): pl.pallas_call(functools.partial(exchange_kernel, scale, batches), out_sh...  59.6 us
    pallas_call x1, Pallas kernels, update(): pl.pallas_call(functools.partial(update_kernel, inv_root, block, starts),...  10.7 us

profile of v1, /device:TPU:0, one launch (start us, length us, event | category | flops | bytes accessed | tf_op | source)
XLA Modules:
  0.0 71.9 jit_solution(3090480768909723099)
XLA Ops:
  0.6 0.0 copy-start
  0.6 0.9 %copy-done = f32[2048,32]{0,1:T(8,128)S(1)} copy-done((f32[2048,32]{0,1:T(8,128)S(1)}, f32[2048,32]{0,1:T(8,128)}, u32[]{:S(2)}) %copy-start) | copy-done | bytes 262168
  1.6 59.6 %exchange.1 = (f32[256,2048]{1,0:T(8,128)S(1)}, f32[2048,1280]{1,0:T(8,128)S(1)}, f32[256,256]{1,0:T(8,128)S(1)}, f32[256,256]{1,0:T(8,128)S(1)}, f32[256,512]{1,0:T(8,128)S(1)}, /*index=5*/f32[256,768]{1,0:T(8,128)S(1)}) custom-call(f32[32,2048]{1,0:T(8,128)S(1)} %bitcast.1, f32[2048,1280]{1,0:T(8,128)} %tin.1), custom_call_target="tpu_custom_call" | custom-call | tf_op jit(solution)/shard_map/exchange/pallas_call | solution.py:297
  61.1 10.7 %update.1 = (f32[256,256]{1,0:T(8,128)}, f32[2048,256]{1,0:T(8,128)}, f32[256,1280]{1,0:T(8,128)}, f32[2048,1280]{1,0:T(8,128)}) custom-call(f32[256,2048]{1,0:T(8,128)S(1)} %get-tuple-element.10.pt, f32[2048,1280]{1,0:T(8,128)S(1)} %get-tuple-element.11.tv, f32[256,256]{1,0:T(8,128)S(1)} %get-tuple-element.12.u, f32[256,256]{1,0:T(8,128)S(1)} %get-tuple-element.13.x, ...), custom_call_target="tpu_custom_call" | custom-call | tf_op jit(solution)/shard_map/update/pallas_call | solution.py:359
Async XLA Ops:
  0.6 1.0 %copy-start = (f32[2048,32]{0,1:T(8,128)S(1)}, f32[2048,32]{0,1:T(8,128)}, u32[]{:S(2)}) copy-start(f32[2048,32]{0,1:T(8,128)} %param.2) | copy-start | bytes 786436

commit v2 on v1

v2 whole, which is shorter than its diff:
```python
import functools
import math

import jax
import jax.numpy as jnp
from jax import lax
from jax.experimental import pallas as pl
from jax.experimental.pallas import tpu as pltpu
from jax.sharding import PartitionSpec as P

F32 = jnp.float32
BF16 = jnp.bfloat16
NN = (((1,), (0,)), ((), ()))
NT = (((1,), (1,)), ((), ()))
TN = (((0,), (0,)), ((), ()))
BLOCK = 32
TILE = 256
dot = functools.partial(lax.dot_general, preferred_element_type=F32)


def split2(x):
    high = x.astype(BF16)
    return high, (x - high.astype(F32)).astype(BF16)


def split3(x):
    high = x.astype(BF16)
    rest = x - high.astype(F32)
    middle = rest.astype(BF16)
    return high, middle, (rest - middle.astype(F32)).astype(BF16)


def left3(x):
    high, low = split2(x)
    return jnp.concatenate([high, low, high], axis=1)


def right3(x, axis=0):
    high, low = split2(x)
    return jnp.concatenate([high, high, low], axis=axis)


def eliminate(r, at):
    groups = BLOCK // 8
    rows = lax.broadcasted_iota(jnp.int32, (8, 128), 0)
    base = (at // 128) * 128
    d = r[:, base : base + 128]
    cols = []
    for q in range(BLOCK):
        lane = at - base + q
        cols.append(
            {
                g: jnp.broadcast_to(d[8 * g : 8 * g + 8, lane : lane + 1], (8, 128))
                for g in range(q // 8, groups)
            }
        )
    width = r.shape[1] // 128
    rr = [
        [r[8 * g : 8 * g + 8, 128 * c : 128 * c + 128] for c in range(width)]
        for g in range(groups)
    ]

    def spread(v, s):
        return jnp.broadcast_to(v[s : s + 1, :], (8, 128))

    for p in range(BLOCK):
        gp, sp = p // 8, p % 8
        inverse = lax.rsqrt(spread(cols[p][gp], sp))
        column = {g: cols[p][g] * inverse for g in range(gp, groups)}
        for q in range(p + 1, BLOCK):
            b = spread(column[q // 8], q % 8)
            for g in range(q // 8, groups):
                cols[q][g] = cols[q][g] - column[g] * b
        below = dict(column)
        below[gp] = jnp.where(rows > sp, column[gp], 0.0)
        for c in range(width):
            row = spread(rr[gp][c], sp) * inverse
            for g in range(gp, groups):
                new = rr[g][c] - below[g] * row
                rr[g][c] = jnp.where(rows == sp, row, new) if g == gp else new
    return jnp.concatenate([jnp.concatenate(x, axis=1) for x in rr], axis=0)


def factor_stage(k, n, m_ref, u_ref, x_ref):
    o = k * BLOCK
    e = o + BLOCK
    r = eliminate(m_ref[o:e, :], o)
    at_row = lax.broadcasted_iota(jnp.int32, (BLOCK, n), 0) + o
    at_col = lax.broadcasted_iota(jnp.int32, (BLOCK, n), 1)
    u_ref[o:e, :] = jnp.where(at_col >= at_row, r[:, :n], 0.0)
    x_ref[o:e, :] = r[:, n:]
    if e < n:
        a0 = (e // 128) * 128
        h, m, l = split3(r)
        left = jnp.concatenate([h, h, m, h, l, m], axis=0)[:, a0:n]
        right = jnp.concatenate([h, m, h, l, h, m], axis=0)
        m_ref[e:n, :] = m_ref[e:n, :] - dot(left, right, TN)[e - a0 :, :]


def exchange_kernel(
    scale, pan, tin, pt, tv, u, x, wf, th, tl, ph, gb, gr, gf, m, wl, w4, r1, r2, r3, r4,
    t_sem, own_sem, ps, pr, gs, grs, es, er, ws, wr,
):
    n, rows = pt.shape
    width = pan.shape[0]
    half = width // 2
    tc = tv.shape[1]
    part = tc // 2
    row, col = lax.axis_index("row"), lax.axis_index("col")
    y, xx = row // 4, row % 4
    z, core = col // 2, col % 2
    up, down, far = lax.rem(z + 1, 4), lax.rem(z + 3, 4), lax.rem(z + 2, 4)
    peer_up = (row, 2 * up + core)
    peer_down = (row, 2 * down + core)
    peer_core = (row, 2 * z + 1 - core)
    peers = (
        (4 * y + xx + 1 - 2 * (xx % 2), col),
        (4 * y + 3 - xx, col),
        (4 * (y + 1 - 2 * (y % 2)) + xx, col),
        (4 * (3 - y) + xx, col),
    )
    bits = ((xx + 1) // 2 % 2, xx // 2, (y + 1) // 2 % 2, y // 2)
    orders = ((0, 1, 2, 3), (1, 0, 3, 2), (2, 3, 0, 1), (3, 2, 1, 0))
    mesh = pl.DeviceIdType.MESH

    quarter = rows // 4
    loads = [
        pltpu.make_async_copy(tin.at[pl.ds(i * quarter, quarter)], tv.at[pl.ds(i * quarter, quarter)], t_sem.at[i])
        for i in range(4)
    ]
    own = pltpu.make_async_copy(pan, pt.at[pl.ds(width * col, width)], own_sem)
    own.start()
    barrier = pltpu.get_barrier_semaphore()
    for peer in (peer_up, peer_down, peer_core, *peers):
        pl.semaphore_signal(barrier, inc=1, device_id=peer, device_id_type=mesh)
    pl.semaphore_wait(barrier, 7)

    sent = []

    def send(src, dst, ssem, rsem, peer):
        copy = pltpu.make_async_remote_copy(src, dst, ssem, rsem, device_id=peer, device_id_type=mesh)
        copy.start()
        sent.append(copy)
        return copy

    def piece(c, side):
        return pt.at[pl.ds(width * c + half * side, half)]

    def forward(index, c, side, peer):
        return send(piece(c, side), piece(c, side), ps.at[index], pr.at[index], peer)

    p0 = send(pan.at[pl.ds(0, half)], piece(col, 0), ps.at[0], pr.at[0], peer_up)
    m0 = send(pan.at[pl.ds(half, half)], piece(col, 1), ps.at[1], pr.at[1], peer_down)
    p1 = send(pan.at[pl.ds(half, half)], piece(col, 1), ps.at[2], pr.at[2], peer_up)
    m1 = send(pan.at[pl.ds(0, half)], piece(col, 0), ps.at[3], pr.at[3], peer_down)
    c0 = send(pan, pt.at[pl.ds(width * col, width)], ps.at[4], pr.at[4], peer_core)
    for load in loads:
        load.start()
    c_down, c_up, c_far = 2 * down + core, 2 * up + core, 2 * far + core

    starts = [pl.multiple_of(2 * width * q, 64) for q in (z, down, up, far)]
    tall = 2 * width

    def split_panel(b):
        at = pl.ds(starts[b], tall)
        ph[0, at], ph[1, at] = split2(pt[at])

    def product(bs, j):
        cols = slice(TILE * j, TILE * j + TILE)
        high = [ph[0, pl.ds(starts[b], tall)] for b in bs]
        low = [ph[1, pl.ds(starts[b], tall)] for b in bs]
        size = tall * len(bs)
        both = dot(jnp.concatenate(high + low, axis=0), th[:, cols], NN)
        total = both[:size] + (both[size:] + dot(jnp.concatenate(high, axis=0), tl[:, cols], NN))
        for i, b in enumerate(bs):
            wl[b, :, cols] = total[tall * i : tall * i + tall]

    keep_row = [pl.multiple_of(16 * s + 8 * bits[orders[s][0]], 8) for s in range(4)]
    give_row = [pl.multiple_of(16 * s + 8 - 8 * bits[orders[s][0]], 8) for s in range(4)]
    keep_col = [pl.multiple_of(part * bits[orders[s][1]], 128) for s in range(4)]
    give_col = [pl.multiple_of(part - part * bits[orders[s][1]], 128) for s in range(4)]
    axes = (0, 1, 2, 3, 1, 0)
    flights = {}

    def product_send(b, level):
        copies = []
        for s in range(4):
            slot = pl.ds(8 * s, 8)
            kept, lanes = pl.ds(keep_row[s], 8), pl.ds(keep_col[s], part)
            final = pl.ds(pl.multiple_of(starts[b] + keep_row[s], 8), 8)
            if level == 0:
                src, dst = wl.at[b, pl.ds(give_row[s], 8)], r1.at[b, slot]
            elif level == 1:
                src, dst = wl.at[b, kept, pl.ds(give_col[s], part)], r2.at[b, slot]
            elif level == 2:
                src, dst = wl.at[b, kept, lanes], r3.at[b, slot]
            elif level == 3:
                src, dst = w4.at[b, slot], r4.at[b, slot]
            elif level == 4:
                src = dst = wf.at[final, lanes]
            else:
                src = dst = wf.at[final]
            copies.append(send(src, dst, ws.at[b, level, s], wr.at[b, level, s], peers[orders[s][axes[level]]]))
        flights[b, level] = copies

    def product_step(b, level):
        for s in range(4):
            flights[b, level][s].wait_recv()
            slot = slice(8 * s, 8 * s + 8)
            kept, lanes = pl.ds(keep_row[s], 8), pl.ds(keep_col[s], part)
            final = pl.ds(pl.multiple_of(starts[b] + keep_row[s], 8), 8)
            if level == 0:
                wl[b, kept] = wl[b, kept] + r1[b, slot]
            elif level == 1:
                wl[b, kept, lanes] = wl[b, kept, lanes] + r2[b, slot]
            elif level == 2:
                w4[b, slot] = wl[b, kept, lanes] + r3[b, slot]
            elif level == 3:
                wf[final, lanes] = w4[b, slot] + r4[b, slot]
        if level < 5:
            product_send(b, level + 1)

    deep = n // 2
    piled = deep // 4
    half_at = pl.multiple_of(deep * core, deep)

    def gram_local():
        high, low = ph[0, pl.ds(half_at, deep)], ph[1, pl.ds(half_at, deep)]
        both = dot(jnp.concatenate([high, low], axis=0), ph[0], NT)
        gb[0] = (both[:deep] + (both[deep:] + dot(high, ph[1], NT))) * scale

    def gram_send(step):
        return [
            send(
                gb.at[step, pl.ds(piled * s, piled)], gr.at[step, pl.ds(piled * s, piled)],
                gs.at[step, s], grs.at[step, s], peers[orders[s][step]],
            )
            for s in range(4)
        ]

    def gram_add(step, copies):
        for s in range(4):
            at = slice(piled * s, piled * s + piled)
            copies[s].wait_recv()
            total = gb[step, at] + gr[step, at]
            if step < 3:
                gb[step + 1, at] = total
            else:
                gf[pl.ds(pl.multiple_of(half_at + piled * s, piled), piled)] = total

    own.wait()
    c0.wait_recv()
    split_panel(0)
    p0.wait_recv()
    p2 = forward(5, c_down, 0, peer_up)
    f1 = forward(6, c_down, 0, peer_core)
    m0.wait_recv()
    m2 = forward(7, c_up, 1, peer_down)
    f2 = forward(8, c_up, 1, peer_core)
    for i in range(4):
        loads[i].wait()

        @pl.loop(0, quarter // 64)
        def _(k, i=i):
            at = pl.ds(pl.multiple_of(i * quarter + k * 64, 64), 64)
            th[at], tl[at] = split2(tv[at])

    for j in range(tc // TILE):
        product((0,), j)
    product_send(0, 0)
    p1.wait_recv()
    f3 = forward(9, c_down, 1, peer_core)
    m1.wait_recv()
    f4 = forward(10, c_up, 0, peer_core)
    for copy in (f1, f2, f3, f4):
        copy.wait_recv()
    split_panel(1)
    split_panel(2)
    p2.wait_recv()
    f5 = forward(11, c_far, 0, peer_core)
    m2.wait_recv()
    f6 = forward(12, c_far, 1, peer_core)
    f5.wait_recv()
    f6.wait_recv()
    split_panel(3)
    gram_local()
    copies = gram_send(0)
    product_step(0, 0)
    for j in range(4):
        product((1, 2), j)
    gram_add(0, copies)
    copies = gram_send(1)
    product_step(0, 1)
    product((1, 2), 4)
    product_send(1, 0)
    product_send(2, 0)
    product((3,), 0)
    product((3,), 1)
    product((3,), 2)
    gram_add(1, copies)
    copies = gram_send(2)
    product((3,), 3)
    product((3,), 4)
    product_send(3, 0)
    product_step(0, 2)
    product_step(1, 0)
    gram_add(2, copies)
    copies = gram_send(3)
    product_step(2, 0)
    product_step(0, 3)
    gram_add(3, copies)
    mine = gf.at[pl.ds(half_at, deep)]
    swap = send(mine, mine, es, er, peer_core)
    product_step(3, 0)
    ri = lax.broadcasted_iota(jnp.int32, (n, n), 0)
    ci = lax.broadcasted_iota(jnp.int32, (n, n), 1)
    m[:, n:] = jnp.where(ri == ci, 1.0, 0.0).astype(F32)
    swap.wait_recv()
    m[:, :n] = gf[...]

    events = [
        (1, 1), (2, 1), (0, 4), (3, 1), (1, 2), (2, 2), (0, 5), (3, 2), (1, 3), (2, 3), (3, 3), (1, 4), (2, 4), (3, 4),
        (1, 5), (2, 5), (3, 5),
    ]
    stages = n // BLOCK
    done = 0
    for k in range(stages):
        factor_stage(k, n, m, u, x)
        goal = (len(events) * (k + 1)) // stages
        while done < goal:
            product_step(*events[done])
            done += 1
    for copy in sent:
        copy.wait_send()


def exchange(panel_t, trailing, scale):
    width, rows = panel_t.shape
    n = width * 8
    tc = trailing.shape[1]
    vm = pltpu.VMEM
    dma = pltpu.SemaphoreType.DMA
    return pl.pallas_call(
        functools.partial(exchange_kernel, scale),
        out_shape=(vm((n, rows), F32), vm((rows, tc), F32), vm((n, n), F32), vm((n, n), F32), vm((n, tc), F32)),
        in_specs=[pl.BlockSpec(memory_space=pltpu.HBM)] * 2,
        out_specs=(pl.BlockSpec(memory_space=pltpu.VMEM),) * 5,
        scratch_shapes=[
            vm((rows, tc), BF16),
            vm((rows, tc), BF16),
            vm((2, n, rows), BF16),
            vm((4, n // 2, n), F32),
            vm((4, n // 2, n), F32),
            vm((n, n), F32),
            vm((n, 2 * n), F32),
            vm((4, 2 * width, tc), F32),
            vm((4, 32, tc // 2), F32),
            vm((4, 32, tc), F32),
            vm((4, 32, tc // 2), F32),
            vm((4, 32, tc // 2), F32),
            vm((4, 32, tc // 2), F32),
            dma((4,)),
            dma,
            dma((13,)),
            dma((13,)),
            dma((4, 4)),
            dma((4, 4)),
            dma,
            dma,
            dma((4, 6, 4)),
            dma((4, 6, 4)),
        ],
        compiler_params=pltpu.CompilerParams(
            collective_id=0, has_side_effects=True, vmem_limit_bytes=36 * 2**20
        ),
        name="exchange",
    )(panel_t, trailing)


def update_kernel(inv_root, block, pt, tv, u, x, w, u_out, q_out, r_out, t_out, r3, x3):
    i = pl.program_id(0)

    @pl.when(i == 0)
    def _():
        left = left3(x[...])
        x3[...] = right3(x[...].T)
        for c in range(0, w.shape[1], TILE):
            r = dot(left, right3(w[:, c : c + TILE]), NN) * inv_root
            r_out[:, c : c + TILE] = r
            r3[:, c : c + TILE] = right3(r * inv_root)
        u_out[...] = u[...]

    at = pl.ds(pl.multiple_of(i * block, block), block)
    q = dot(left3(pt[:, at].T), x3[...], NN)
    q_out[...] = q
    q3 = left3(q)
    for c in range(0, r_out.shape[1], TILE):
        t_out[:, c : c + TILE] = tv[at, c : c + TILE] - dot(q3, r3[:, c : c + TILE], NN)


def update(pt, tv, u, x, w, inv_root, block=256):
    n, rows = pt.shape
    tc = tv.shape[1]
    resident = pl.BlockSpec(memory_space=pltpu.VMEM)

    def whole(*shape):
        return pl.BlockSpec(shape, lambda i: (0, 0))

    def by_rows(width):
        return pl.BlockSpec((block, width), lambda i: (i, 0))

    return pl.pallas_call(
        functools.partial(update_kernel, inv_root, block),
        grid=(rows // block,),
        out_shape=(
            jax.ShapeDtypeStruct((n, n), F32),
            jax.ShapeDtypeStruct((rows, n), F32),
            jax.ShapeDtypeStruct((n, tc), F32),
            jax.ShapeDtypeStruct((rows, tc), F32),
        ),
        in_specs=[resident] * 5,
        out_specs=(whole(n, n), by_rows(n), whole(n, tc), by_rows(tc)),
        scratch_shapes=[pltpu.VMEM((3 * n, tc), BF16), pltpu.VMEM((3 * n, n), BF16)],
        compiler_params=pltpu.CompilerParams(vmem_limit_bytes=20 * 2**20),
        name="update",
    )(pt, tv, u, x, w)


def per_device(panel, trailing_in):
    rows_all = panel.shape[0] * lax.axis_size("row")
    pt, tv, u, x, w = exchange(panel.T, trailing_in, 1.0 / rows_all)
    return update(pt, tv, u, x, w, 1.0 / math.sqrt(rows_all))


def solution(mesh):
    in_specs = (P("row", "col"), P("row", "col"))
    out_specs = (P(), P("row", None), P(None, "col"), P("row", "col"))
    return jax.shard_map(
        per_device, mesh=mesh, in_specs=in_specs, out_specs=out_specs, check_vma=False
    )
```

time: 72 us -> 67.9 us (0.943)
  Pallas kernels: 70.3 us -> 66.2 us
    pallas_call x2, Pallas kernels: 70.3 us -> 66.2 us  [the longest x1 55.5 us: exchange(): pl.pallas_call(functools.partial(exchange_kernel, scale), out_shape=(vm((...]
where the time goes in v2:
time: 67.9 us; the launch traced here: 67.8 us
  Pallas kernels  66.2 us (97%)
  local copies, waits for them, and re-layouts  0.94 us (1%)
    pallas_call x1, Pallas kernels, exchange(): pl.pallas_call(functools.partial(exchange_kernel, scale), out_shape=(vm((...  55.5 us
    pallas_call x1, Pallas kernels, update(): pl.pallas_call(functools.partial(update_kernel, inv_root, block), grid=(r...  10.7 us

profile of v2, /device:TPU:0, one launch (start us, length us, event | category | flops | bytes accessed | tf_op | source)
XLA Modules:
  0.0 67.8 jit_solution(12064933692600401570)
XLA Ops:
  0.6 0.0 copy-start
  0.6 0.9 %copy-done = f32[2048,32]{0,1:T(8,128)S(1)} copy-done((f32[2048,32]{0,1:T(8,128)S(1)}, f32[2048,32]{0,1:T(8,128)}, u32[]{:S(2)}) %copy-start) | copy-done | bytes 262168
  1.6 55.5 %exchange.1 = (f32[256,2048]{1,0:T(8,128)S(1)}, f32[2048,1280]{1,0:T(8,128)S(1)}, f32[256,256]{1,0:T(8,128)S(1)}, f32[256,256]{1,0:T(8,128)S(1)}, f32[256,1280]{1,0:T(8,128)S(1)}) custom-call(f32[32,2048]{1,0:T(8,128)S(1)} %bitcast.1, f32[2048,1280]{1,0:T(8,128)} %tin.1), custom_call_target="tpu_custom_call" | custom-call | tf_op jit(solution)/shard_map/exchange/pallas_call | solution.py:343
  57.0 10.7 %update.1 = (f32[256,256]{1,0:T(8,128)}, f32[2048,256]{1,0:T(8,128)}, f32[256,1280]{1,0:T(8,128)}, f32[2048,1280]{1,0:T(8,128)}) custom-call(f32[256,2048]{1,0:T(8,128)S(1)} %get-tuple-element.9.pt, f32[2048,1280]{1,0:T(8,128)S(1)} %get-tuple-element.10.tv, f32[256,256]{1,0:T(8,128)S(1)} %get-tuple-element.11.u, f32[256,256]{1,0:T(8,128)S(1)} %get-tuple-element.12.x, ...), custom_call_target="tpu_custom_call" | custom-call | tf_op jit(solution)/shard_map/update/pallas_call | solution.py:412
Async XLA Ops:
  0.6 1.0 %copy-start = (f32[2048,32]{0,1:T(8,128)S(1)}, f32[2048,32]{0,1:T(8,128)}, u32[]{:S(2)}) copy-start(f32[2048,32]{0,1:T(8,128)} %param.2) | copy-start | bytes 786436

commit v3 on v2

--- a/solution.py
+++ b/solution.py
@@ -98,14 +98,13 @@
 
 
 def exchange_kernel(
-    scale, pan, tin, pt, tv, u, x, wf, th, tl, ph, gb, gr, gf, m, wl, w4, r1, r2, r3, r4,
+    scale, pan, tin, pt, tv, u, x, wf, th, tl, ph, g1, g2, gf, m, wl, r1, r2,
     t_sem, own_sem, ps, pr, gs, grs, es, er, ws, wr,
 ):
     n, rows = pt.shape
     width = pan.shape[0]
     half = width // 2
     tc = tv.shape[1]
-    part = tc // 2
     row, col = lax.axis_index("row"), lax.axis_index("col")
     y, xx = row // 4, row % 4
     z, core = col // 2, col % 2
@@ -113,14 +112,13 @@
     peer_up = (row, 2 * up + core)
     peer_down = (row, 2 * down + core)
     peer_core = (row, 2 * z + 1 - core)
-    peers = (
-        (4 * y + xx + 1 - 2 * (xx % 2), col),
-        (4 * y + 3 - xx, col),
-        (4 * (y + 1 - 2 * (y % 2)) + xx, col),
-        (4 * (3 - y) + xx, col),
-    )
-    bits = ((xx + 1) // 2 % 2, xx // 2, (y + 1) // 2 % 2, y // 2)
-    orders = ((0, 1, 2, 3), (1, 0, 3, 2), (2, 3, 0, 1), (3, 2, 1, 0))
+    place = (xx, y)
+
+    def on_ring(axis, ahead):
+        if axis == 0:
+            return (4 * y + lax.rem(xx + ahead, 4), col)
+        return (4 * lax.rem(y + ahead, 4) + xx, col)
+
     mesh = pl.DeviceIdType.MESH
 
     quarter = rows // 4
@@ -131,9 +129,10 @@
     own = pltpu.make_async_copy(pan, pt.at[pl.ds(width * col, width)], own_sem)
     own.start()
     barrier = pltpu.get_barrier_semaphore()
-    for peer in (peer_up, peer_down, peer_core, *peers):
+    around = [on_ring(axis, ahead) for axis in (0, 1) for ahead in (1, 2, 3)]
+    for peer in (peer_up, peer_down, peer_core, *around):
         pl.semaphore_signal(barrier, inc=1, device_id=peer, device_id_type=mesh)
-    pl.semaphore_wait(barrier, 7)
+    pl.semaphore_wait(barrier, 9)
 
     sent = []
 
@@ -175,78 +174,72 @@
         for i, b in enumerate(bs):
             wl[b, :, cols] = total[tall * i : tall * i + tall]
 
-    keep_row = [pl.multiple_of(16 * s + 8 * bits[orders[s][0]], 8) for s in range(4)]
-    give_row = [pl.multiple_of(16 * s + 8 - 8 * bits[orders[s][0]], 8) for s in range(4)]
-    keep_col = [pl.multiple_of(part * bits[orders[s][1]], 128) for s in range(4)]
-    give_col = [pl.multiple_of(part - part * bits[orders[s][1]], 128) for s in range(4)]
-    axes = (0, 1, 2, 3, 1, 0)
+    short = 8
     flights = {}
 
-    def product_send(b, level):
+    def product_send(b, phase):
         copies = []
-        for s in range(4):
-            slot = pl.ds(8 * s, 8)
-            kept, lanes = pl.ds(keep_row[s], 8), pl.ds(keep_col[s], part)
-            final = pl.ds(pl.multiple_of(starts[b] + keep_row[s], 8), 8)
-            if level == 0:
-                src, dst = wl.at[b, pl.ds(give_row[s], 8)], r1.at[b, slot]
-            elif level == 1:
-                src, dst = wl.at[b, kept, pl.ds(give_col[s], part)], r2.at[b, slot]
-            elif level == 2:
-                src, dst = wl.at[b, kept, lanes], r3.at[b, slot]
-            elif level == 3:
-                src, dst = w4.at[b, slot], r4.at[b, slot]
-            elif level == 4:
-                src = dst = wf.at[final, lanes]
-            else:
-                src = dst = wf.at[final]
-            copies.append(send(src, dst, ws.at[b, level, s], wr.at[b, level, s], peers[orders[s][axes[level]]]))
-        flights[b, level] = copies
-
-    def product_step(b, level):
-        for s in range(4):
-            flights[b, level][s].wait_recv()
-            slot = slice(8 * s, 8 * s + 8)
-            kept, lanes = pl.ds(keep_row[s], 8), pl.ds(keep_col[s], part)
-            final = pl.ds(pl.multiple_of(starts[b] + keep_row[s], 8), 8)
-            if level == 0:
-                wl[b, kept] = wl[b, kept] + r1[b, slot]
-            elif level == 1:
-                wl[b, kept, lanes] = wl[b, kept, lanes] + r2[b, slot]
-            elif level == 2:
-                w4[b, slot] = wl[b, kept, lanes] + r3[b, slot]
-            elif level == 3:
-                wf[final, lanes] = w4[b, slot] + r4[b, slot]
-        if level < 5:
-            product_send(b, level + 1)
+        for h in (0, 1):
+            axis = (h + phase) % 2
+            first = pl.multiple_of(starts[b] + 32 * h + short * place[h], short)
+            for ahead in (2, 1, 3):
+                there = lax.rem(place[axis] + ahead, 4)
+                if phase == 0:
+                    src = wl.at[b, pl.ds(pl.multiple_of(32 * h + short * there, short), short)]
+                    dst = r1.at[b, h, ahead - 1]
+                elif phase == 1:
+                    src = dst = r2.at[b, h, place[axis]]
+                else:
+                    src = dst = wf.at[pl.ds(first, short)]
+                ssem, rsem = ws.at[b, phase, h, ahead - 1], wr.at[b, phase, h, ahead - 1]
+                copies.append(send(src, dst, ssem, rsem, on_ring(axis, ahead)))
+        flights[b, phase] = copies
+
+    def product_step(b, phase):
+        for copy in flights[b, phase]:
+            copy.wait_recv()
+        for h in (0, 1):
+            first = pl.multiple_of(starts[b] + 32 * h + short * place[h], short)
+            if phase == 0:
+                mine = wl[b, pl.ds(pl.multiple_of(32 * h + short * place[h], short), short)]
+                r2[b, h, place[1 - h]] = (mine + r1[b, h, 0]) + (r1[b, h, 1] + r1[b, h, 2])
+            elif phase == 1:
+                wf[pl.ds(first, short)] = (r2[b, h, 0] + r2[b, h, 1]) + (r2[b, h, 2] + r2[b, h, 3])
+        if phase < 2:
+            product_send(b, phase + 1)
 
     deep = n // 2
-    piled = deep // 4
+    piled = deep // 2
     half_at = pl.multiple_of(deep * core, deep)
+    gram = (g1, g2)
 
     def gram_local():
         high, low = ph[0, pl.ds(half_at, deep)], ph[1, pl.ds(half_at, deep)]
         both = dot(jnp.concatenate([high, low], axis=0), ph[0], NT)
-        gb[0] = (both[:deep] + (both[deep:] + dot(high, ph[1], NT))) * scale
-
-    def gram_send(step):
-        return [
-            send(
-                gb.at[step, pl.ds(piled * s, piled)], gr.at[step, pl.ds(piled * s, piled)],
-                gs.at[step, s], grs.at[step, s], peers[orders[s][step]],
-            )
-            for s in range(4)
-        ]
-
-    def gram_add(step, copies):
-        for s in range(4):
-            at = slice(piled * s, piled * s + piled)
-            copies[s].wait_recv()
-            total = gb[step, at] + gr[step, at]
-            if step < 3:
-                gb[step + 1, at] = total
+        total = (both[:deep] + (both[deep:] + dot(high, ph[1], NT))) * scale
+        for h in (0, 1):
+            g1[h, place[h]] = total[piled * h : piled * h + piled]
+
+    def gram_send(phase):
+        copies = []
+        for h in (0, 1):
+            axis = (h + phase) % 2
+            for ahead in (2, 1, 3):
+                mine = gram[phase].at[h, place[axis]]
+                ssem, rsem = gs.at[phase, h, ahead - 1], grs.at[phase, h, ahead - 1]
+                copies.append(send(mine, mine, ssem, rsem, on_ring(axis, ahead)))
+        return copies
+
+    def gram_add(phase, copies):
+        for copy in copies:
+            copy.wait_recv()
+        for h in (0, 1):
+            g = gram[phase]
+            total = (g[h, 0] + g[h, 1]) + (g[h, 2] + g[h, 3])
+            if phase == 0:
+                g2[h, place[1 - h]] = total
             else:
-                gf[pl.ds(pl.multiple_of(half_at + piled * s, piled), piled)] = total
+                gf[pl.ds(pl.multiple_of(half_at + piled * h, piled), piled)] = total
 
     own.wait()
     c0.wait_recv()
@@ -276,52 +269,41 @@
         copy.wait_recv()
     split_panel(1)
     split_panel(2)
+    for j in range(3):
+        product((1, 2), j)
     p2.wait_recv()
     f5 = forward(11, c_far, 0, peer_core)
     m2.wait_recv()
     f6 = forward(12, c_far, 1, peer_core)
+    for j in range(3, tc // TILE):
+        product((1, 2), j)
     f5.wait_recv()
     f6.wait_recv()
     split_panel(3)
     gram_local()
     copies = gram_send(0)
+    product_send(1, 0)
+    product_send(2, 0)
     product_step(0, 0)
-    for j in range(4):
-        product((1, 2), j)
+    for j in range(tc // TILE):
+        product((3,), j)
     gram_add(0, copies)
     copies = gram_send(1)
+    product_send(3, 0)
+    product_step(1, 0)
+    product_step(2, 0)
     product_step(0, 1)
-    product((1, 2), 4)
-    product_send(1, 0)
-    product_send(2, 0)
-    product((3,), 0)
-    product((3,), 1)
-    product((3,), 2)
     gram_add(1, copies)
-    copies = gram_send(2)
-    product((3,), 3)
-    product((3,), 4)
-    product_send(3, 0)
-    product_step(0, 2)
-    product_step(1, 0)
-    gram_add(2, copies)
-    copies = gram_send(3)
-    product_step(2, 0)
-    product_step(0, 3)
-    gram_add(3, copies)
     mine = gf.at[pl.ds(half_at, deep)]
     swap = send(mine, mine, es, er, peer_core)
-    product_step(3, 0)
     ri = lax.broadcasted_iota(jnp.int32, (n, n), 0)
     ci = lax.broadcasted_iota(jnp.int32, (n, n), 1)
     m[:, n:] = jnp.where(ri == ci, 1.0, 0.0).astype(F32)
+    product_step(3, 0)
     swap.wait_recv()
     m[:, :n] = gf[...]
 
-    events = [
-        (1, 1), (2, 1), (0, 4), (3, 1), (1, 2), (2, 2), (0, 5), (3, 2), (1, 3), (2, 3), (3, 3), (1, 4), (2, 4), (3, 4),
-        (1, 5), (2, 5), (3, 5),
-    ]
+    events = [(1, 1), (2, 1), (0, 2), (3, 1), (1, 2), (2, 2), (3, 2)]
     stages = n // BLOCK
     done = 0
     for k in range(stages):
@@ -349,26 +331,23 @@
             vm((rows, tc), BF16),
             vm((rows, tc), BF16),
             vm((2, n, rows), BF16),
-            vm((4, n // 2, n), F32),
-            vm((4, n // 2, n), F32),
+            vm((2, 4, n // 4, n), F32),
+            vm((2, 4, n // 4, n), F32),
             vm((n, n), F32),
             vm((n, 2 * n), F32),
             vm((4, 2 * width, tc), F32),
-            vm((4, 32, tc // 2), F32),
-            vm((4, 32, tc), F32),
-            vm((4, 32, tc // 2), F32),
-            vm((4, 32, tc // 2), F32),
-            vm((4, 32, tc // 2), F32),
+            vm((4, 2, 3, 8, tc), F32),
+            vm((4, 2, 4, 8, tc), F32),
             dma((4,)),
             dma,
             dma((13,)),
             dma((13,)),
-            dma((4, 4)),
-            dma((4, 4)),
+            dma((2, 2, 3)),
+            dma((2, 2, 3)),
             dma,
             dma,
-            dma((4, 6, 4)),
-            dma((4, 6, 4)),
+            dma((4, 3, 2, 3)),
+            dma((4, 3, 2, 3)),
         ],
         compiler_params=pltpu.CompilerParams(
             collective_id=0, has_side_effects=True, vmem_limit_bytes=36 * 2**20
@@ -377,41 +356,40 @@
     )(panel_t, trailing)
 
 
-def update_kernel(inv_root, block, pt, tv, u, x, w, u_out, q_out, r_out, t_out, r3, x3):
-    i = pl.program_id(0)
+def update_kernel(inv_root, pt, tv, u, x, w, u_out, q_out, r_out, t_out, q3, r3, x3):
+    i, j = pl.program_id(0), pl.program_id(1)
+    block, tile = t_out.shape
+    rows = pl.ds(pl.multiple_of(i * block, block), block)
+    cols = pl.ds(pl.multiple_of(j * tile, tile), tile)
+
+    @pl.when((i == 0) & (j == 0))
+    def _():
+        x3[...] = right3(x[...].T)
+        u_out[...] = u[...]
 
     @pl.when(i == 0)
     def _():
-        left = left3(x[...])
-        x3[...] = right3(x[...].T)
-        for c in range(0, w.shape[1], TILE):
-            r = dot(left, right3(w[:, c : c + TILE]), NN) * inv_root
-            r_out[:, c : c + TILE] = r
-            r3[:, c : c + TILE] = right3(r * inv_root)
-        u_out[...] = u[...]
-
-    at = pl.ds(pl.multiple_of(i * block, block), block)
-    q = dot(left3(pt[:, at].T), x3[...], NN)
-    q_out[...] = q
-    q3 = left3(q)
-    for c in range(0, r_out.shape[1], TILE):
-        t_out[:, c : c + TILE] = tv[at, c : c + TILE] - dot(q3, r3[:, c : c + TILE], NN)
-
-
-def update(pt, tv, u, x, w, inv_root, block=256):
+        r = dot(left3(x[...]), right3(w[:, cols]), NN) * inv_root
+        r_out[...] = r
+        r3[:, cols] = right3(r * inv_root)
+
+    @pl.when(j == 0)
+    def _():
+        q = dot(left3(pt[:, rows].T), x3[...], NN)
+        q_out[...] = q
+        q3[...] = left3(q)
+
+    t_out[...] = tv[rows, cols] - dot(q3[...], r3[:, cols], NN)
+
+
+def update(pt, tv, u, x, w, inv_root, block=512):
     n, rows = pt.shape
     tc = tv.shape[1]
+    tiles = tc // TILE
     resident = pl.BlockSpec(memory_space=pltpu.VMEM)
-
-    def whole(*shape):
-        return pl.BlockSpec(shape, lambda i: (0, 0))
-
-    def by_rows(width):
-        return pl.BlockSpec((block, width), lambda i: (i, 0))
-
     return pl.pallas_call(
-        functools.partial(update_kernel, inv_root, block),
-        grid=(rows // block,),
+        functools.partial(update_kernel, inv_root),
+        grid=(rows // block, tiles),
         out_shape=(
             jax.ShapeDtypeStruct((n, n), F32),
             jax.ShapeDtypeStruct((rows, n), F32),
@@ -419,8 +397,17 @@
             jax.ShapeDtypeStruct((rows, tc), F32),
         ),
         in_specs=[resident] * 5,
-        out_specs=(whole(n, n), by_rows(n), whole(n, tc), by_rows(tc)),
-        scratch_shapes=[pltpu.VMEM((3 * n, tc), BF16), pltpu.VMEM((3 * n, n), BF16)],
+        out_specs=(
+            pl.BlockSpec((n, n), lambda i, j: (0, 0)),
+            pl.BlockSpec((block, n), lambda i, j: (i, 0)),
+            pl.BlockSpec((n, TILE), lambda i, j: (0, jnp.where(i == 0, j, tiles - 1))),
+            pl.BlockSpec((block, TILE), lambda i, j: (i, j)),
+        ),
+        scratch_shapes=[
+            pltpu.VMEM((block, 3 * n), BF16),
+            pltpu.VMEM((3 * n, tc), BF16),
+            pltpu.VMEM((3 * n, n), BF16),
+        ],
         compiler_params=pltpu.CompilerParams(vmem_limit_bytes=20 * 2**20),
         name="update",
     )(pt, tv, u, x, w)

time: 67.9 us -> 68.5 us (level)
    pallas_call x1, Pallas kernels: 10.7 us -> 14.6 us  [update(): pl.pallas_call(functools.partial(update_kernel, inv_root), grid=(rows //...]
    pallas_call x1, Pallas kernels: 55.5 us -> 51.8 us  [exchange(): pl.pallas_call(functools.partial(exchange_kernel, scale), out_shape=(vm((...]
where the time goes in v3:
time: 68.5 us; the launch traced here: 68 us
  Pallas kernels  66.4 us (97%)
  local copies, waits for them, and re-layouts  0.94 us (1%)
    pallas_call x1, Pallas kernels, exchange(): pl.pallas_call(functools.partial(exchange_kernel, scale), out_shape=(vm((...  51.8 us
    pallas_call x1, Pallas kernels, update(): pl.pallas_call(functools.partial(update_kernel, inv_root), grid=(rows //...  14.6 us

profile of v3, /device:TPU:0, one launch (start us, length us, event | category | flops | bytes accessed | tf_op | source)
XLA Modules:
  0.0 68.0 jit_solution(6316535435788385684)
XLA Ops:
  0.6 0.0 copy-start
  0.6 0.9 %copy-done = f32[2048,32]{0,1:T(8,128)S(1)} copy-done((f32[2048,32]{0,1:T(8,128)S(1)}, f32[2048,32]{0,1:T(8,128)}, u32[]{:S(2)}) %copy-start) | copy-done | bytes 262168
  1.6 51.8 %exchange.1 = (f32[256,2048]{1,0:T(8,128)S(1)}, f32[2048,1280]{1,0:T(8,128)S(1)}, f32[256,256]{1,0:T(8,128)S(1)}, f32[256,256]{1,0:T(8,128)S(1)}, f32[256,1280]{1,0:T(8,128)S(1)}) custom-call(f32[32,2048]{1,0:T(8,128)S(1)} %bitcast.1, f32[2048,1280]{1,0:T(8,128)} %tin.1), custom_call_target="tpu_custom_call" | custom-call | tf_op jit(solution)/shard_map/exchange/pallas_call | solution.py:325
  53.4 14.6 %update.1 = (f32[256,256]{1,0:T(8,128)}, f32[2048,256]{1,0:T(8,128)}, f32[256,1280]{1,0:T(8,128)}, f32[2048,1280]{1,0:T(8,128)}) custom-call(f32[256,2048]{1,0:T(8,128)S(1)} %get-tuple-element.9.pt, f32[2048,1280]{1,0:T(8,128)S(1)} %get-tuple-element.10.tv, f32[256,256]{1,0:T(8,128)S(1)} %get-tuple-element.11.u, f32[256,256]{1,0:T(8,128)S(1)} %get-tuple-element.12.x, ...), custom_call_target="tpu_custom_call" | custom-call | tf_op jit(solution)/shard_map/update/pallas_call | solution.py:390
Async XLA Ops:
  0.6 1.0 %copy-start = (f32[2048,32]{0,1:T(8,128)S(1)}, f32[2048,32]{0,1:T(8,128)}, u32[]{:S(2)}) copy-start(f32[2048,32]{0,1:T(8,128)} %param.2) | copy-start | bytes 786436

commit v4 on v3

--- a/solution.py
+++ b/solution.py
@@ -98,7 +98,7 @@
 
 
 def exchange_kernel(
-    scale, pan, tin, pt, tv, u, x, wf, th, tl, ph, g1, g2, gf, m, wl, r1, r2,
+    scale, pan, tin, p3, tv, u, x, wf, pt, th, tl, ph, g1, g2, gf, m, wl, r1, r2,
     t_sem, own_sem, ps, pr, gs, grs, es, er, ws, wr,
 ):
     n, rows = pt.shape
@@ -275,24 +275,32 @@
     f5 = forward(11, c_far, 0, peer_core)
     m2.wait_recv()
     f6 = forward(12, c_far, 1, peer_core)
+    product_step(0, 0)
     for j in range(3, tc // TILE):
         product((1, 2), j)
+    product_send(1, 0)
+    product_send(2, 0)
     f5.wait_recv()
     f6.wait_recv()
     split_panel(3)
     gram_local()
     copies = gram_send(0)
-    product_send(1, 0)
-    product_send(2, 0)
-    product_step(0, 0)
+    product_step(0, 1)
     for j in range(tc // TILE):
         product((3,), j)
+    product_step(1, 0)
+    product_step(2, 0)
     gram_add(0, copies)
     copies = gram_send(1)
     product_send(3, 0)
-    product_step(1, 0)
-    product_step(2, 0)
-    product_step(0, 1)
+
+    @pl.loop(0, rows // TILE)
+    def _(k):
+        at = pl.ds(pl.multiple_of(k * TILE, TILE), TILE)
+        p3[at] = left3(pt[:, at].T)
+
+    product_step(1, 1)
+    product_step(2, 1)
     gram_add(1, copies)
     mine = gf.at[pl.ds(half_at, deep)]
     swap = send(mine, mine, es, er, peer_core)
@@ -303,7 +311,7 @@
     swap.wait_recv()
     m[:, :n] = gf[...]
 
-    events = [(1, 1), (2, 1), (0, 2), (3, 1), (1, 2), (2, 2), (3, 2)]
+    events = [(0, 2), (3, 1), (1, 2), (2, 2), (3, 2)]
     stages = n // BLOCK
     done = 0
     for k in range(stages):
@@ -324,10 +332,11 @@
     dma = pltpu.SemaphoreType.DMA
     return pl.pallas_call(
         functools.partial(exchange_kernel, scale),
-        out_shape=(vm((n, rows), F32), vm((rows, tc), F32), vm((n, n), F32), vm((n, n), F32), vm((n, tc), F32)),
+        out_shape=(vm((rows, 3 * n), BF16), vm((rows, tc), F32), vm((n, n), F32), vm((n, n), F32), vm((n, tc), F32)),
         in_specs=[pl.BlockSpec(memory_space=pltpu.HBM)] * 2,
         out_specs=(pl.BlockSpec(memory_space=pltpu.VMEM),) * 5,
         scratch_shapes=[
+            vm((n, rows), F32),
             vm((rows, tc), BF16),
             vm((rows, tc), BF16),
             vm((2, n, rows), BF16),
@@ -356,40 +365,36 @@
     )(panel_t, trailing)
 
 
-def update_kernel(inv_root, pt, tv, u, x, w, u_out, q_out, r_out, t_out, q3, r3, x3):
-    i, j = pl.program_id(0), pl.program_id(1)
-    block, tile = t_out.shape
+def update_kernel(inv_root, p3, tv, u, x, w, u_out, q_out, r_out, t_out, r3, x3):
+    i = pl.program_id(0)
+    block = q_out.shape[0]
     rows = pl.ds(pl.multiple_of(i * block, block), block)
-    cols = pl.ds(pl.multiple_of(j * tile, tile), tile)
-
-    @pl.when((i == 0) & (j == 0))
+    tiles = range(0, r_out.shape[1], TILE)
+
+    @pl.when(i == 0)
     def _():
         x3[...] = right3(x[...].T)
+        left = left3(x[...])
+        for c in tiles:
+            r = dot(left, right3(w[:, c : c + TILE]), NN) * inv_root
+            r_out[:, c : c + TILE] = r
+            r3[:, c : c + TILE] = right3(r * inv_root)
         u_out[...] = u[...]
 
-    @pl.when(i == 0)
-    def _():
-        r = dot(left3(x[...]), right3(w[:, cols]), NN) * inv_root
-        r_out[...] = r
-        r3[:, cols] = right3(r * inv_root)
-
-    @pl.when(j == 0)
-    def _():
-        q = dot(left3(pt[:, rows].T), x3[...], NN)
-        q_out[...] = q
-        q3[...] = left3(q)
-
-    t_out[...] = tv[rows, cols] - dot(q3[...], r3[:, cols], NN)
-
-
-def update(pt, tv, u, x, w, inv_root, block=512):
-    n, rows = pt.shape
-    tc = tv.shape[1]
-    tiles = tc // TILE
+    q = dot(p3[rows], x3[...], NN)
+    q_out[...] = q
+    q3 = left3(q)
+    for c in tiles:
+        t_out[:, c : c + TILE] = tv[rows, c : c + TILE] - dot(q3, r3[:, c : c + TILE], NN)
+
+
+def update(p3, tv, u, x, w, inv_root, block=512):
+    rows, tc = tv.shape
+    n = u.shape[0]
     resident = pl.BlockSpec(memory_space=pltpu.VMEM)
     return pl.pallas_call(
         functools.partial(update_kernel, inv_root),
-        grid=(rows // block, tiles),
+        grid=(rows // block,),
         out_shape=(
             jax.ShapeDtypeStruct((n, n), F32),
             jax.ShapeDtypeStruct((rows, n), F32),
@@ -398,25 +403,21 @@
         ),
         in_specs=[resident] * 5,
         out_specs=(
-            pl.BlockSpec((n, n), lambda i, j: (0, 0)),
-            pl.BlockSpec((block, n), lambda i, j: (i, 0)),
-            pl.BlockSpec((n, TILE), lambda i, j: (0, jnp.where(i == 0, j, tiles - 1))),
-            pl.BlockSpec((block, TILE), lambda i, j: (i, j)),
+            pl.BlockSpec((n, n), lambda i: (0, 0)),
+            pl.BlockSpec((block, n), lambda i: (i, 0)),
+            pl.BlockSpec((n, tc), lambda i: (0, 0)),
+            pl.BlockSpec((block, tc), lambda i: (i, 0)),
         ),
-        scratch_shapes=[
-            pltpu.VMEM((block, 3 * n), BF16),
-            pltpu.VMEM((3 * n, tc), BF16),
-            pltpu.VMEM((3 * n, n), BF16),
-        ],
+        scratch_shapes=[pltpu.VMEM((3 * n, tc), BF16), pltpu.VMEM((3 * n, n), BF16)],
         compiler_params=pltpu.CompilerParams(vmem_limit_bytes=20 * 2**20),
         name="update",
-    )(pt, tv, u, x, w)
+    )(p3, tv, u, x, w)
 
 
 def per_device(panel, trailing_in):
     rows_all = panel.shape[0] * lax.axis_size("row")
-    pt, tv, u, x, w = exchange(panel.T, trailing_in, 1.0 / rows_all)
-    return update(pt, tv, u, x, w, 1.0 / math.sqrt(rows_all))
+    p3, tv, u, x, w = exchange(panel.T, trailing_in, 1.0 / rows_all)
+    return update(p3, tv, u, x, w, 1.0 / math.sqrt(rows_all))
 
 
 def solution(mesh):

time: 68.5 us -> 62.9 us (0.918)
  Pallas kernels: 66.4 us -> 61.2 us
    pallas_call x1, Pallas kernels: 14.6 us -> 9.43 us  [update(): pl.pallas_call(functools.partial(update_kernel, inv_root), grid=(rows //...]
where the time goes in v4:
time: 62.9 us; the launch traced here: 62.7 us
  Pallas kernels  61.2 us (97%)
  local copies, waits for them, and re-layouts  0.94 us (1%)
  between operations  0.65 us (1%)
    pallas_call x1, Pallas kernels, exchange(): pl.pallas_call(functools.partial(exchange_kernel, scale), out_shape=(vm((...  51.7 us
    pallas_call x1, Pallas kernels, update(): pl.pallas_call(functools.partial(update_kernel, inv_root), grid=(rows //...  9.43 us

profile of v4, /device:TPU:0, one launch (start us, length us, event | category | flops | bytes accessed | tf_op | source)
XLA Modules:
  0.0 62.7 jit_solution(15923308950628391560)
XLA Ops:
  0.6 0.0 copy-start
  0.6 0.9 %copy-done = f32[2048,32]{0,1:T(8,128)S(1)} copy-done((f32[2048,32]{0,1:T(8,128)S(1)}, f32[2048,32]{0,1:T(8,128)}, u32[]{:S(2)}) %copy-start) | copy-done | bytes 262168
  1.6 51.7 %exchange.1 = (bf16[2048,768]{1,0:T(8,128)(2,1)S(1)}, f32[2048,1280]{1,0:T(8,128)S(1)}, f32[256,256]{1,0:T(8,128)S(1)}, f32[256,256]{1,0:T(8,128)S(1)}, f32[256,1280]{1,0:T(8,128)S(1)}) custom-call(f32[32,2048]{1,0:T(8,128)S(1)} %bitcast.1, f32[2048,1280]{1,0:T(8,128)} %tin.1), custom_call_target="tpu_custom_call" | custom-call | tf_op jit(solution)/shard_map/exchange/pallas_call | solution.py:333
  53.3 9.4 %update.1 = (f32[256,256]{1,0:T(8,128)}, f32[2048,256]{1,0:T(8,128)}, f32[256,1280]{1,0:T(8,128)}, f32[2048,1280]{1,0:T(8,128)}) custom-call(bf16[2048,768]{1,0:T(8,128)(2,1)S(1)} %get-tuple-element.9.p3, f32[2048,1280]{1,0:T(8,128)S(1)} %get-tuple-element.10.tv, f32[256,256]{1,0:T(8,128)S(1)} %get-tuple-element.11.u, f32[256,256]{1,0:T(8,128)S(1)} %get-tuple-element.12.x, ...), custom_call_target="tpu_custom_call" | custom-call | tf_op jit(solution)/shard_map/update/pallas_call | solution.py:395
Async XLA Ops:
  0.6 1.0 %copy-start = (f32[2048,32]{0,1:T(8,128)S(1)}, f32[2048,32]{0,1:T(8,128)}, u32[]{:S(2)}) copy-start(f32[2048,32]{0,1:T(8,128)} %param.2) | copy-start | bytes 786436

commit v5 on v4

--- a/solution.py
+++ b/solution.py
@@ -416,7 +416,7 @@
 
 def per_device(panel, trailing_in):
     rows_all = panel.shape[0] * lax.axis_size("row")
-    p3, tv, u, x, w = exchange(panel.T, trailing_in, 1.0 / rows_all)
+    p3, tv, u, x, w = exchange(pltpu.with_memory_space_constraint(panel.T, pltpu.HBM), trailing_in, 1.0 / rows_all)
     return update(p3, tv, u, x, w, 1.0 / math.sqrt(rows_all))
 
 

time: 62.9 us -> 62.2 us (0.989)
  local copies, waits for them, and re-layouts: 0.94 us -> 0 us
    unnamed x2 -> x0, local copies, waits for them, and re-layouts: 0.94 us -> none
where the time goes in v5:
time: 62.2 us; the launch traced here: 62.1 us
  Pallas kernels  61.4 us (99%)
  between operations  0.64 us (1%)
    pallas_call x1, Pallas kernels, exchange(): pl.pallas_call(functools.partial(exchange_kernel, scale), out_shape=(vm((...  52 us
    pallas_call x1, Pallas kernels, update(): pl.pallas_call(functools.partial(update_kernel, inv_root), grid=(rows //...  9.44 us

profile of v5, /device:TPU:0, one launch (start us, length us, event | category | flops | bytes accessed | tf_op | source)
XLA Modules:
  0.0 62.1 jit_solution(9332940035252698613)
XLA Ops:
  0.6 52.0 %exchange.1 = (bf16[2048,768]{1,0:T(8,128)(2,1)S(1)}, f32[2048,1280]{1,0:T(8,128)S(1)}, f32[256,256]{1,0:T(8,128)S(1)}, f32[256,256]{1,0:T(8,128)S(1)}, f32[256,1280]{1,0:T(8,128)S(1)}) custom-call(f32[32,2048]{1,0:T(8,128)} %bitcast.1, f32[2048,1280]{1,0:T(8,128)} %tin.1), custom_call_target="tpu_custom_call" | custom-call | tf_op jit(solution)/shard_map/exchange/pallas_call | solution.py:333
  52.7 9.4 %update.1 = (f32[256,256]{1,0:T(8,128)}, f32[2048,256]{1,0:T(8,128)}, f32[256,1280]{1,0:T(8,128)}, f32[2048,1280]{1,0:T(8,128)}) custom-call(bf16[2048,768]{1,0:T(8,128)(2,1)S(1)} %get-tuple-element.9.p3, f32[2048,1280]{1,0:T(8,128)S(1)} %get-tuple-element.10.tv, f32[256,256]{1,0:T(8,128)S(1)} %get-tuple-element.11.u, f32[256,256]{1,0:T(8,128)S(1)} %get-tuple-element.12.x, ...), custom_call_target="tpu_custom_call" | custom-call | tf_op jit(solution)/shard_map/update/pallas_call | solution.py:395
